TPU v7x, 128 devices: a whole 4x4x4 slice. The times are simulated.
128 devices in a mesh: gx: 4 (over y), gy: 32 (over z, x, core).
Axes of the slice: x: 4, y: 4, z: 4, core: 2. Of those that a mesh axis runs over, the one named last changes fastest.
Arguments:
- positions: float32 [3, 2097152], P(None, ('gx', 'gy')), may hold values from -6 to 6
- normals: float32 [3, 2097152], P(None, ('gx', 'gy')), may hold values from -6 to 6
- areas: float32 [2097152], P(('gx', 'gy')), may hold values from 0.5 to 2
- pair_first: int32 [16384], P(('gx', 'gy')), may hold values from 0 to 8191, as said below
- pair_second: int32 [16384], P(('gx', 'gy')), may hold values from 0 to 8191, as said below
- pair_count: int32 [128], P(('gx', 'gy')), may hold values from 32 to 128, as said below
Outputs:
- gradient: float32 [3, 2097152], P(None, ('gx', 'gy'))
Inputs may be any that keep to these rules, and one draw needn't show every extreme that they name: `pair_first`: slot s holds a first cluster owned by device s // 128, that is in s // 128 * 64 to (s // 128 + 1) * 64 - 1. `pair_second`: the second cluster of slot s lies on a device at most 2 away from s // 128: its index // 64 differs from s // 128 by at most 2. Dead slots hold such pairs too. `pair_count`: some device has all 128 slots live in every draw.
All inputs are finite; a program needn't handle non-finite values.
Results may differ from a plain program's by a relative error of at most 0.0001.
Values sent between devices are 32-bit elements; how exact they have to be, the bound alone decides.
A program may use at most 64 MiB of HBM per device.

v0:
```python
import jax
import jax.numpy as jnp
from jax import lax
from jax.sharding import PartitionSpec as P

C = 256
REACH = 2
BLOCK = 4


def with_halo(block, sides, width):
    for axis, dim in sides:
        count = lax.axis_size(axis)
        forward = [(i, i + 1) for i in range(count - 1)]
        backward = [(target, source) for source, target in forward]
        low = lax.ppermute(
            lax.slice_in_dim(block, block.shape[dim] - width, None, axis=dim), axis, forward
        )
        high = lax.ppermute(lax.slice_in_dim(block, 0, width, axis=dim), axis, backward)
        block = jnp.concatenate([low, block, high], axis=dim)
    return block


def from_behind(value, axis, by):
    size = lax.axis_size(axis)
    pairs = [(i, i + by) for i in range(size) if 0 <= i + by < size]
    return lax.ppermute(value, axis, pairs)


def tile_terms(pos_f, nor_f, area_f, pos_g, nor_g, area_g):
    delta = [pos_f[:, k, :, None] - pos_g[:, k, None, :] for k in range(3)]
    radius = delta[0] * delta[0] + delta[1] * delta[1] + delta[2] * delta[2] + 1.0
    inverse = 1.0 / radius
    weight = area_f[:, :, None] * area_g[:, None, :] * inverse * inverse * inverse
    along_f = (
        nor_f[:, 0, :, None] * delta[0]
        + nor_f[:, 1, :, None] * delta[1]
        + nor_f[:, 2, :, None] * delta[2]
    )
    along_g = (
        nor_g[:, 0, None, :] * delta[0]
        + nor_g[:, 1, None, :] * delta[1]
        + nor_g[:, 2, None, :] * delta[2]
    )
    linear_f = 2.0 * weight * along_f
    linear_g = 2.0 * weight * along_g
    radial = -6.0 * weight * inverse * (along_f * along_f + along_g * along_g)
    grad_first = []
    grad_second = []
    for k in range(3):
        comp = linear_f * nor_f[:, k, :, None] + linear_g * nor_g[:, k, None, :] + radial * delta[k]
        grad_first.append(jnp.sum(comp, axis=2))
        grad_second.append(-jnp.sum(comp, axis=1))
    return (jnp.stack(grad_first, axis=1), jnp.stack(grad_second, axis=1))


def body(positions, normals, areas, pair_first, pair_second, pair_count):
    faces = areas.shape[0]
    clusters = faces // C
    span = 2 * REACH + 1
    geometry = jnp.concatenate([positions, normals, areas[None, :]], axis=0)
    lefts = []
    rights = []
    for distance in range(REACH):
        if distance == 0:
            operand = geometry
        else:
            operand = jnp.concatenate([rights[-1], lefts[-1]], axis=1)
        extended = with_halo(operand, ((("gx", "gy"), 1),), faces)
        lefts.append(extended[:, :faces])
        rights.append(extended[:, extended.shape[1] - faces :])
    window = jnp.concatenate(lefts[::-1] + [geometry] + rights, axis=1)
    window = window.reshape(7, span * clusters, C).transpose(1, 0, 2)
    where_pos = window[:, 0:3, :]
    where_nor = window[:, 3:6, :]
    where_area = window[:, 6, :]
    device_index = lax.axis_index(("gx", "gy"))
    base = device_index * clusters
    first_slot = REACH * clusters + pair_first - base
    owner = pair_second // clusters
    second_slot = (owner - device_index + REACH) * clusters + pair_second % clusters
    count = pair_count[0]

    def run_block(index, accum):
        start = index * BLOCK
        first = lax.dynamic_slice_in_dim(first_slot, start, BLOCK)
        second = lax.dynamic_slice_in_dim(second_slot, start, BLOCK)
        alive = (start + jnp.arange(BLOCK, dtype=jnp.int32) < count).astype(jnp.float32)
        grad_first, grad_second = tile_terms(
            where_pos[first],
            where_nor[first],
            where_area[first],
            where_pos[second],
            where_nor[second],
            where_area[second],
        )
        targets = jnp.concatenate([first, second])
        weights = jnp.concatenate([alive, alive])
        terms = jnp.concatenate([grad_first, grad_second], axis=0) * weights[:, None, None]
        return accum.at[targets].add(terms)

    accum = jnp.zeros((span * clusters, 3, C), jnp.float32)
    upper = (count + BLOCK - 1) // BLOCK
    accum = lax.fori_loop(0, upper, run_block, accum)
    owned = accum[REACH * clusters : (REACH + 1) * clusters]
    for offset in range(-REACH, REACH + 1):
        if offset != 0:
            piece = accum[(offset + REACH) * clusters : (offset + REACH + 1) * clusters]
            owned = owned + from_behind(piece, ("gx", "gy"), offset)
    return owned.transpose(1, 0, 2).reshape(3, faces)


def solution(mesh):
    in_specs = (
        P(None, ("gx", "gy")),
        P(None, ("gx", "gy")),
        P(("gx", "gy")),
        P(("gx", "gy")),
        P(("gx", "gy")),
        P(("gx", "gy")),
    )
    out_specs = P(None, ("gx", "gy"))
    return jax.shard_map(body, mesh=mesh, in_specs=in_specs, out_specs=out_specs, check_vma=False)
```

profile of v0, /device:TPU:10, one launch (start us, length us, event | category | flops | bytes accessed | tf_op | source)
XLA Modules:
  0.0 415.1 jit_solution(9554869547942453984)
XLA Ops:
  3.2 3.6 collective-permute-start.2
  6.8 4.9 %collective-permute-done = f32[7,16384]{1,0:T(8,128)S(1)} collective-permute-done((f32[7,16384]{1,0:T(8,128)S(1)}, f32[7,16384]{1,0:T(8,128)S(1)}, u32[]{:S(2)}, u32[]{:S(2)}) %collective-permute-start) | collective-permute-done | bytes 458784 | tf_op jit(solution)/shard_map/ppermute | solution.py:16
  15.0 3.6 collective-permute-start.3
  18.7 3.5 collective-permute-done.1
  27.5 354.9 %while.10 = (s32[]{:T(128)}, f32[320,3,256]{2,1,0:T(4,128)S(1)}, s32[]{:T(128)}, s32[128]{0:T(128)S(1)}, s32[128]{0:T(128)S(1)}, /*index=5*/f32[320,256]{1,0:T(8...) while((s32[]{:T(128)}, f32[320,3,256]{2,1,0:T(4,128)S(1)}, ...), condition=%wide.region_8.9_spmd, body=%wide.region_0.8_spmd.sunk | while | flops 14197846 | bytes 598591 | solution.py:104
  56.1 3.0 fusion.43
  78.2 3.0 fusion.43
  100.4 3.0 fusion.43
  122.6 3.0 fusion.43
  144.8 3.0 fusion.43
  155.9 3.0 fusion.43
  178.1 3.0 fusion.43
  211.3 3.0 fusion.43
  233.5 3.0 fusion.43
  244.6 3.0 fusion.43
  266.8 3.0 fusion.43
  300.1 3.0 fusion.43
  322.3 3.0 fusion.43
  333.3 3.0 fusion.43
  344.4 3.0 fusion.43
  366.6 3.0 fusion.43
  384.6 16.7 %collective-permute-start.5 = (f32[64,3,256]{2,1,0:T(4,128)S(1)}, f32[64,3,256]{2,1,0:T(4,128)S(1)}, u32[]{:S(2)}, u32[]{:S(2)}) collective-permute-start(f32[64,3,256]{2,1,0:T(4,128)S(1)} %get-tuple-element.101), channel_id=1, source_target_pairs={{1,0},{2,1},{3,2},{4,3},{5,4},{6,5},{7,6},{8,7},{9,8},{10,9},{11,1... | collective-permute-start | bytes 589832 | tf_op jit(solution)/shard_map/ppermute | solution.py:27
  405.2 4.1 collective-permute-done.6
  409.3 5.0 %collective-permute-done.7 = f32[64,3,256]{2,1,0:T(4,128)S(1)} collective-permute-done((f32[64,3,256]{2,1,0:T(4,128)S(1)}, f32[64,3,256]{2,1,0:T(4,128)S(1)}, u32[]{:S(2)}, u32[]{:S(2)}) %collective-permute-start.7) | collective-permute-done | bytes 196640 | tf_op jit(solution)/shard_map/ppermute | solution.py:27
  (1126 shorter events, 318.7 us)
Async XLA Ops:
  1.2 10.5 %collective-permute-start = (f32[7,16384]{1,0:T(8,128)S(1)}, f32[7,16384]{1,0:T(8,128)S(1)}, u32[]{:S(2)}, u32[]{:S(2)}) collective-permute-start(f32[7,16384]{1,0:T(8,128)S(1)} %pad_maximum_fusion), channel_id=1, source_target_pairs={{0,1},{1,2},{2,3},{3,4},{4,5},{5,6},{6,7},{7,8},{8,9},{9,10},{10,1... | collective-permute-start | bytes 1376264 | tf_op jit(solution)/shard_map/ppermute | solution.py:16
  3.2 11.9 %collective-permute-start.2 = (f32[7,16384]{1,0:T(8,128)S(1)}, f32[7,16384]{1,0:T(8,128)S(1)}, u32[]{:S(2)}, u32[]{:S(2)}) collective-permute-start(f32[7,16384]{1,0:T(8,128)S(1)} %pad_maximum_fusion), channel_id=1, source_target_pairs={{1,0},{2,1},{3,2},{4,3},{5,4},{6,5},{7,6},{8,7},{9,8},{10,9},{11,1... | collective-permute-start | bytes 1376264 | tf_op jit(solution)/shard_map/ppermute | solution.py:19
  11.7 10.5 %collective-permute-start.1 = (f32[7,16384]{1,0:T(8,128)S(1)}, f32[7,16384]{1,0:T(8,128)S(1)}, u32[]{:S(2)}, u32[]{:S(2)}) collective-permute-start(f32[7,16384]{1,0:T(8,128)S(1)} %collective-permute-done), channel_id=1, source_target_pairs={{0,1},{1,2},{2,3},{3,4},{4,5},{5,6},{6,7},{7,8},{8,9},{9,10},{10,1... | collective-permute-start | bytes 1376264 | tf_op jit(solution)/shard_map/ppermute | solution.py:16
  15.0 10.3 %collective-permute-start.3 = (f32[7,16384]{1,0:T(8,128)S(1)}, f32[7,16384]{1,0:T(8,128)S(1)}, u32[]{:S(2)}, u32[]{:S(2)}) collective-permute-start(f32[7,16384]{1,0:T(8,128)S(1)} %collective-permute-done.2), channel_id=1, source_target_pairs={{1,0},{2,1},{3,2},{4,3},{5,4},{6,5},{7,6},{8,7},{9,8},{10,9},{11,1... | collective-permute-start | bytes 1376264 | tf_op jit(solution)/shard_map/ppermute | solution.py:19
  382.6 22.5 %collective-permute-start.4 = (f32[64,3,256]{2,1,0:T(4,128)S(1)}, f32[64,3,256]{2,1,0:T(4,128)S(1)}, u32[]{:S(2)}, u32[]{:S(2)}) collective-permute-start(f32[64,3,256]{2,1,0:T(4,128)S(1)} %get-tuple-element.98), channel_id=1, source_target_pairs={{2,0},{3,1},{4,2},{5,3},{6,4},{7,5},{8,6},{9,7},{10,8},{11,9},{12,... | collective-permute-start | bytes 589832 | tf_op jit(solution)/shard_map/ppermute | solution.py:27
  384.6 20.6 %collective-permute-start.5 = (f32[64,3,256]{2,1,0:T(4,128)S(1)}, f32[64,3,256]{2,1,0:T(4,128)S(1)}, u32[]{:S(2)}, u32[]{:S(2)}) collective-permute-start(f32[64,3,256]{2,1,0:T(4,128)S(1)} %get-tuple-element.101), channel_id=1, source_target_pairs={{1,0},{2,1},{3,2},{4,3},{5,4},{6,5},{7,6},{8,7},{9,8},{10,9},{11,1... | collective-permute-start | bytes 589832 | tf_op jit(solution)/shard_map/ppermute | solution.py:27
  401.3 8.0 %collective-permute-start.6 = (f32[64,3,256]{2,1,0:T(4,128)S(1)}, f32[64,3,256]{2,1,0:T(4,128)S(1)}, u32[]{:S(2)}, u32[]{:S(2)}) collective-permute-start(f32[64,3,256]{2,1,0:T(4,128)S(1)} %get-tuple-element.100), channel_id=1, source_target_pairs={{0,1},{1,2},{2,3},{3,4},{4,5},{5,6},{6,7},{7,8},{8,9},{9,10},{10,1... | collective-permute-start | bytes 589832 | tf_op jit(solution)/shard_map/ppermute | solution.py:27
  403.2 11.1 %collective-permute-start.7 = (f32[64,3,256]{2,1,0:T(4,128)S(1)}, f32[64,3,256]{2,1,0:T(4,128)S(1)}, u32[]{:S(2)}, u32[]{:S(2)}) collective-permute-start(f32[64,3,256]{2,1,0:T(4,128)S(1)} %get-tuple-element.99), channel_id=1, source_target_pairs={{0,2},{1,3},{2,4},{3,5},{4,6},{5,7},{6,8},{7,9},{8,10},{9,11},{10,... | collective-permute-start | bytes 589832 | tf_op jit(solution)/shard_map/ppermute | solution.py:27
where the time goes:
time: 422 us; the launch traced here: 415 us
  local copies, waits for them, and re-layouts  199 us (47%)
  other arithmetic  155 us (37%)
  starting transfers between devices  33.6 us (8%)
  waiting for transfers between devices  20.6 us (5%)
  loops' own time  6.29 us (1%)
    reduce_sum x32, other arithmetic, tile_terms(): grad_first.append(jnp.sum(comp, axis=2))  95.5 us
    gather x32, local copies, waits for them, and re-layouts, run_block(): where_pos[second]  60.4 us
    gather x32, local copies, waits for them, and re-layouts, run_block(): where_pos[first]  60.4 us
    scatter-add x32, other arithmetic, run_block(): return accum.at[targets].add(terms)  25.1 us
    ppermute x4, starting transfers between devices, from_behind(): return lax.ppermute(value, axis, pairs)  22.5 us
    lt x32, other arithmetic, run_block(): start + jnp.arange(BLOCK, dtype=jnp.int32) < count  20.9 us
    gather x32, local copies, waits for them, and re-layouts, run_block(): where_nor[second]  18.3 us
    gather x32, local copies, waits for them, and re-layouts, run_block(): where_nor[first]  18.3 us
  transfers between devices with their start and end apart: 8, of which 5 were waited for; matrix products, arithmetic and copies ran while one was open for 0% of the time, Pallas kernels for 0%

commit v1 on v0

v1 whole, which is shorter than its diff:
```python
import jax
import jax.numpy as jnp
from jax import lax
from jax.experimental import pallas as pl
from jax.experimental.pallas import tpu as pltpu
from jax.sharding import PartitionSpec as P

C = 256
REACH = 2
F32 = jnp.float32
BF = jnp.bfloat16


def split3(t):
    a = t.astype(BF).astype(F32)
    r = t - a
    b = r.astype(BF).astype(F32)
    return a, b, r - b


def split2(t):
    a = t.astype(BF).astype(F32)
    return a, t - a


def wide(v):
    return jnp.broadcast_to(v, (8, C))


def prep(f, g, alive, lhs_ref, rhs_ref, wf_ref, wg_ref, keep_ref):
    row = lax.broadcasted_iota(jnp.int32, (8, C), 0)
    isp = row < 3
    isn = (row >= 3) & (row < 6)
    ctr = jnp.where(isp, wide(jnp.sum(f, axis=1, keepdims=True) * (1.0 / C)), 0.0)
    f = f - ctr
    g = g - ctr

    def dots(t):
        p = jnp.where(isp, t, 0.0)
        n = jnp.where(isp, pltpu.roll(t, 5, 0), 0.0)
        return p, n, wide(jnp.sum(p * p, axis=0, keepdims=True)), wide(jnp.sum(p * n, axis=0, keepdims=True))

    pf, nf, sf, cf = dots(f)
    pg, ng, sg, cg = dots(g)
    one = jnp.ones((8, C), F32)
    zero = jnp.zeros((8, C), F32)
    a0, a1, a2 = split3(jnp.where(row < 6, f, jnp.where(row == 6, sf + 1.0, cf)))
    lhs_ref[...] = jnp.concatenate([a0, a0, a0, a1, a1, a2, one, zero], axis=0).T.astype(BF)
    tr = jnp.where(isp, -2.0 * g, jnp.where(row == 6, 1.0, 0.0))
    ts = jnp.where(isn, -pltpu.roll(g, 3, 0), jnp.where(row == 7, 1.0, 0.0))

    def rows3(u):
        return jnp.where(row == 0, u[0], jnp.where(row == 1, u[1], jnp.where(row == 2, u[2], 0.0)))

    lasts = (rows3(split3(sg)), zero, rows3(split3(-cg)))
    for j, t in enumerate((tr, ts, ng)):
        u0, u1, u2 = split3(t)
        rhs_ref[:, j * C : (j + 1) * C] = jnp.concatenate([u0, u1, u2, u0, u1, u0, lasts[j], zero], axis=0).astype(BF)
    af = wide(f[6:7, :])
    ag = wide(g[6:7, :])
    af2 = af * (2.0 * alive)
    ag2 = ag * (2.0 * alive)

    def put(ref, vs):
        for j, v in enumerate(vs):
            ref[j] = jnp.concatenate(split2(v), axis=0).astype(BF)

    put(wf_ref, (nf * af2, jnp.where(row == 3, af2, 0.0), (-3.0 * pf + jnp.where(row == 4, 3.0, 0.0)) * af2))
    put(wg_ref, (jnp.where(row == 3, ag2, 0.0), ng * ag2, (3.0 * pg - jnp.where(row == 4, 3.0, 0.0)) * ag2))
    for i, v in enumerate((nf, pf, af, ng, pg, ag)):
        keep_ref[i] = v


def forward(lhs_ref, rhs_ref, l_ref, rows):
    for i in range(C // rows):
        sl = slice(i * rows, (i + 1) * rows)
        left = lhs_ref[sl, :]
        r2, sf, sg = (jnp.dot(left, rhs_ref[:, j * C : (j + 1) * C], preferred_element_type=F32) for j in range(3))
        inv = 1.0 / r2
        inv3 = inv * inv * inv
        lf = inv3 * sf
        lg = inv3 * sg
        rad = inv * (lf * sf + lg * sg)
        for j, v in enumerate((lf, lg, rad)):
            h = v.astype(BF)
            l_ref[j, sl, :] = h
            l_ref[j + 3, sl, :] = (v - h.astype(F32)).astype(BF)


def sums(l_ref, wf_ref, wg_ref, keep_ref):
    cs = None
    rs = None
    for j in range(6):
        tile = l_ref[j]
        a = lax.dot_general(wf_ref[j % 3], tile, (((1,), (0,)), ((), ())), preferred_element_type=F32)
        b = lax.dot_general(wg_ref[j % 3], tile, (((1,), (1,)), ((), ())), preferred_element_type=F32)
        cs = a if cs is None else cs + a
        rs = b if rs is None else rs + b
    cs = cs[0:8] + cs[8:16]
    rs = rs[0:8] + rs[8:16]
    nf, pf, af, ng, pg, ag = (keep_ref[i] for i in range(6))
    gf = af * (rs + nf * wide(rs[3:4]) + pf * wide(rs[4:5]))
    gg = -ag * (cs + ng * wide(cs[3:4]) + pg * wide(cs[4:5]))
    return gf, gg


def near_field(first, second, count, geos):
    nwin = len(geos)
    faces = geos[0].shape[1]

    def kernel(first, second, count, *refs):
        geo = refs[:nwin]
        outs = refs[nwin : 2 * nwin]
        r = list(refs[2 * nwin :])
        win = r.pop(0)
        acc = r.pop(0)
        bufs = [[r.pop(0) for _ in range(6)] for _ in range(2)]
        sem = r.pop(0)
        copies = [
            pltpu.make_async_copy(geo[k], win.at[:, pl.ds(k * faces, faces)], sem.at[k]) for k in range(nwin)
        ]
        for c in copies:
            c.start()
        acc[...] = jnp.zeros_like(acc)
        for c in copies:
            c.wait()
        n = count[0]

        def ds(c):
            return pl.ds(pl.multiple_of(c * C, C), C)

        def step(i, carry):
            for u in range(2):
                p = 2 * i + u
                prep(win[:, ds(first[p])], win[:, ds(second[p])], jnp.where(p < n, 1.0, 0.0).astype(F32), *bufs[u][:5])
            for u in range(2):
                forward(bufs[u][0], bufs[u][1], bufs[u][5], 32)
            for u in range(2):
                p = 2 * i + u
                gf, gg = sums(bufs[u][5], bufs[u][2], bufs[u][3], bufs[u][4])
                acc[:, ds(first[p])] += gf
                acc[:, ds(second[p])] += gg
            return carry

        lax.fori_loop(0, (n + 1) // 2, step, 0)
        for k in range(nwin):
            outs[k][...] = acc[0:3, k * faces : (k + 1) * faces]

    buf = [
        pltpu.VMEM((C, 64), BF),
        pltpu.VMEM((64, 3 * C), BF),
        pltpu.VMEM((3, 16, C), BF),
        pltpu.VMEM((3, 16, C), BF),
        pltpu.VMEM((6, 8, C), F32),
        pltpu.VMEM((6, C, C), BF),
    ]
    return pl.pallas_call(
        kernel,
        out_shape=[jax.ShapeDtypeStruct((3, faces), F32)] * nwin,
        in_specs=[pl.BlockSpec(memory_space=pltpu.SMEM)] * 3 + [pl.BlockSpec(memory_space=pl.ANY)] * nwin,
        out_specs=[pl.BlockSpec(memory_space=pltpu.VMEM)] * nwin,
        scratch_shapes=[pltpu.VMEM((8, nwin * faces), F32)] * 2 + buf + buf + [pltpu.SemaphoreType.DMA((nwin,))],
        compiler_params=pltpu.CompilerParams(vmem_limit_bytes=40 * 2**20),
    )(first, second, count, *geos)


def shifted(value, axis, by):
    size = 1
    for a in axis:
        size *= lax.axis_size(a)
    return lax.ppermute(value, axis, [(i, i + by) for i in range(size) if 0 <= i + by < size])


def body(positions, normals, areas, pair_first, pair_second, pair_count):
    faces = areas.shape[0]
    clusters = faces // C
    axis = ("gx", "gy")
    geometry = jnp.concatenate([positions, normals, areas[None, :], jnp.zeros((1, faces), F32)], axis=0)
    geos = [geometry if k == 0 else shifted(geometry, axis, -k) for k in range(-REACH, REACH + 1)]
    base = (lax.axis_index(axis) - REACH) * clusters
    outs = near_field(pair_first - base, pair_second - base, pair_count, geos)
    owned = outs[REACH]
    for k in range(-REACH, REACH + 1):
        if k != 0:
            owned = owned + shifted(outs[k + REACH], axis, k)
    return owned


def solution(mesh):
    flat = P(("gx", "gy"))
    deep = P(None, ("gx", "gy"))
    return jax.shard_map(
        body, mesh=mesh, in_specs=(deep, deep, flat, flat, flat, flat), out_specs=deep, check_vma=False
    )
```

time: 422 us -> 128 us (0.30)
  the two profiles are of different devices: /device:TPU:10 before, /device:TPU:113 now
where the time goes in v1:
time: 128 us
  Pallas kernels  76.4 us (60%)
  waiting for transfers between devices  25.1 us (20%)
  starting transfers between devices  22.6 us (18%)
  other arithmetic  2.08 us (2%)
    pallas_call x1, Pallas kernels, near_field(): pl.pallas_call(kernel, out_shape=[jax.ShapeDtypeStruct((3, faces), F32)]...  76.4 us
    ppermute x8, waiting for transfers between devices, shifted(): lax.ppermute(value, axis, [(i, i + by) for i in range(size) if 0 <= i + b...  25.1 us
    ppermute x8, starting transfers between devices, shifted(): lax.ppermute(value, axis, [(i, i + by) for i in range(size) if 0 <= i + b...  22.6 us
  transfers between devices with their start and end apart: 8, of which 4 were waited for; matrix products, arithmetic and copies ran while one was open for 0% of the time, Pallas kernels for 0%

profile of v1, /device:TPU:113, one launch (start us, length us, event | category | flops | bytes accessed | tf_op | source)
XLA Modules:
  0.0 127.7 jit_solution(17730074435240758580)
XLA Ops:
  0.0 0.1 pad.3.clone
  0.1 1.2 maximum_maximum_fusion.refs_2_
  1.3 4.2 %collective-permute-start.3 = (f32[8,16384]{1,0:T(8,128)S(1)}, f32[8,16384]{1,0:T(8,128)S(1)}, u32[]{:S(2)}, u32[]{:S(2)}) collective-permute-start(f32[8,16384]{1,0:T(8,128)S(1)} %maximum_maximum_fusion.refs_2_), channel_id=1, source_target_pairs={{2,0},{3,1},{4,2},{5,3},{6,4},{7,5},{8,6},{9,7},{10,8},{11,9},{12,... | collective-permute-start | bytes 1572872 | tf_op jit(solution)/shard_map/ppermute | solution.py:171
  5.5 2.9 %collective-permute-start.2 = (f32[8,16384]{1,0:T(8,128)S(1)}, f32[8,16384]{1,0:T(8,128)S(1)}, u32[]{:S(2)}, u32[]{:S(2)}) collective-permute-start(f32[8,16384]{1,0:T(8,128)S(1)} %maximum_maximum_fusion.refs_2_), channel_id=1, source_target_pairs={{1,0},{2,1},{3,2},{4,3},{5,4},{6,5},{7,6},{8,7},{9,8},{10,9},{11,1... | collective-permute-start | bytes 1572872 | tf_op jit(solution)/shard_map/ppermute | solution.py:171
  8.4 2.7 %collective-permute-start.1 = (f32[8,16384]{1,0:T(8,128)S(1)}, f32[8,16384]{1,0:T(8,128)S(1)}, u32[]{:S(2)}, u32[]{:S(2)}) collective-permute-start(f32[8,16384]{1,0:T(8,128)S(1)} %maximum_maximum_fusion.refs_2_), channel_id=1, source_target_pairs={{0,1},{1,2},{2,3},{3,4},{4,5},{5,6},{6,7},{7,8},{8,9},{9,10},{10,1... | collective-permute-start | bytes 1572872 | tf_op jit(solution)/shard_map/ppermute | solution.py:171
  11.1 1.9 %collective-permute-start = (f32[8,16384]{1,0:T(8,128)S(1)}, f32[8,16384]{1,0:T(8,128)S(1)}, u32[]{:S(2)}, u32[]{:S(2)}) collective-permute-start(f32[8,16384]{1,0:T(8,128)S(1)} %maximum_maximum_fusion.refs_2_), channel_id=1, source_target_pairs={{0,2},{1,3},{2,4},{3,5},{4,6},{5,7},{6,8},{7,9},{8,10},{9,11},{10,... | collective-permute-start | bytes 1572872 | tf_op jit(solution)/shard_map/ppermute | solution.py:171
  13.7 0.0 copy-start
  13.7 0.0 copy-start.1
  13.7 0.6 copy-done
  14.4 0.0 copy-done.1
  14.4 1.7 %collective-permute-done.3.refs_4_ = f32[8,16384]{1,0:T(8,128)S(1)} collective-permute-done((f32[8,16384]{1,0:T(8,128)S(1)}, f32[8,16384]{1,0:T(8,128)S(1)}, u32[]{:S(2)}, u32[]{:S(2)}) %collective-permute-start.3) | collective-permute-done | bytes 524320 | tf_op jit(solution)/shard_map/ppermute | solution.py:171
  16.1 6.6 %collective-permute-done.2.refs_3_ = f32[8,16384]{1,0:T(8,128)S(1)} collective-permute-done((f32[8,16384]{1,0:T(8,128)S(1)}, f32[8,16384]{1,0:T(8,128)S(1)}, u32[]{:S(2)}, u32[]{:S(2)}) %collective-permute-start.2) | collective-permute-done | bytes 524320 | tf_op jit(solution)/shard_map/ppermute | solution.py:171
  22.8 0.0 collective-permute-done.1.refs_1_
  22.8 8.8 %collective-permute-done.refs_0_ = f32[8,16384]{1,0:T(8,128)S(1)} collective-permute-done((f32[8,16384]{1,0:T(8,128)S(1)}, f32[8,16384]{1,0:T(8,128)S(1)}, u32[]{:S(2)}, u32[]{:S(2)}) %collective-permute-start) | collective-permute-done | bytes 524320 | tf_op jit(solution)/shard_map/ppermute | solution.py:171
  31.6 76.4 %shard_map.64 = (f32[3,16384]{1,0:T(4,128)S(1)}, f32[3,16384]{1,0:T(4,128)S(1)}, f32[3,16384]{1,0:T(4,128)S(1)}, f32[3,16384]{1,0:T(4,128)S(1)}, f32[3,16384]{1,0:T(4,128)S(1)}) custom-call(s32[128]{0:T(128)S(1)} %get-tuple-element.16.first, s32[128]{0:T(128)S(1)} %get-tuple-element.15.second, s32[1]{0:T(128)S(6)} %copy.7.count, ...), custom_call_target="tpu_custom_call" | custom-call | tf_op jit(solution)/shard_map/pallas_call | solution.py:157
  108.0 1.9 %collective-permute-start.4 = (f32[3,16384]{1,0:T(4,128)S(1)}, f32[3,16384]{1,0:T(4,128)S(1)}, u32[]{:S(2)}, u32[]{:S(2)}) collective-permute-start(f32[3,16384]{1,0:T(4,128)S(1)} %get-tuple-element.11), channel_id=1, source_target_pairs={{2,0},{3,1},{4,2},{5,3},{6,4},{7,5},{8,6},{9,7},{10,8},{11,9},{12,... | collective-permute-start | bytes 589832 | tf_op jit(solution)/shard_map/ppermute | solution.py:171
  110.0 1.9 %collective-permute-start.5 = (f32[3,16384]{1,0:T(4,128)S(1)}, f32[3,16384]{1,0:T(4,128)S(1)}, u32[]{:S(2)}, u32[]{:S(2)}) collective-permute-start(f32[3,16384]{1,0:T(4,128)S(1)} %get-tuple-element.12), channel_id=1, source_target_pairs={{1,0},{2,1},{3,2},{4,3},{5,4},{6,5},{7,6},{8,7},{9,8},{10,9},{11,1... | collective-permute-start | bytes 589832 | tf_op jit(solution)/shard_map/ppermute | solution.py:171
  111.9 3.6 %collective-permute-start.6 = (f32[3,16384]{1,0:T(4,128)S(1)}, f32[3,16384]{1,0:T(4,128)S(1)}, u32[]{:S(2)}, u32[]{:S(2)}) collective-permute-start(f32[3,16384]{1,0:T(4,128)S(1)} %get-tuple-element.13), channel_id=1, source_target_pairs={{0,1},{1,2},{2,3},{3,4},{4,5},{5,6},{6,7},{7,8},{8,9},{9,10},{10,1... | collective-permute-start | bytes 589832 | tf_op jit(solution)/shard_map/ppermute | solution.py:171
  115.5 3.4 %collective-permute-start.7 = (f32[3,16384]{1,0:T(4,128)S(1)}, f32[3,16384]{1,0:T(4,128)S(1)}, u32[]{:S(2)}, u32[]{:S(2)}) collective-permute-start(f32[3,16384]{1,0:T(4,128)S(1)} %get-tuple-element.14), channel_id=1, source_target_pairs={{0,2},{1,3},{2,4},{3,5},{4,6},{5,7},{6,8},{7,9},{8,10},{9,11},{10,... | collective-permute-start | bytes 589832 | tf_op jit(solution)/shard_map/ppermute | solution.py:171
  118.9 0.0 collective-permute-done.4
  118.9 0.0 collective-permute-done.5
  118.9 0.0 collective-permute-done.6
  119.0 7.9 %collective-permute-done.7 = f32[3,16384]{1,0:T(4,128)S(1)} collective-permute-done((f32[3,16384]{1,0:T(4,128)S(1)}, f32[3,16384]{1,0:T(4,128)S(1)}, u32[]{:S(2)}, u32[]{:S(2)}) %collective-permute-start.7) | collective-permute-done | bytes 196640 | tf_op jit(solution)/shard_map/ppermute | solution.py:171
  126.8 0.8 add_add_fusion
  (1 shorter events, 0.0 us)
Async XLA Ops:
  1.3 14.8 %collective-permute-start.3 = (f32[8,16384]{1,0:T(8,128)S(1)}, f32[8,16384]{1,0:T(8,128)S(1)}, u32[]{:S(2)}, u32[]{:S(2)}) collective-permute-start(f32[8,16384]{1,0:T(8,128)S(1)} %maximum_maximum_fusion.refs_2_), channel_id=1, source_target_pairs={{2,0},{3,1},{4,2},{5,3},{6,4},{7,5},{8,6},{9,7},{10,8},{11,9},{12,... | collective-permute-start | bytes 1572872 | tf_op jit(solution)/shard_map/ppermute | solution.py:171
  5.5 17.2 %collective-permute-start.2 = (f32[8,16384]{1,0:T(8,128)S(1)}, f32[8,16384]{1,0:T(8,128)S(1)}, u32[]{:S(2)}, u32[]{:S(2)}) collective-permute-start(f32[8,16384]{1,0:T(8,128)S(1)} %maximum_maximum_fusion.refs_2_), channel_id=1, source_target_pairs={{1,0},{2,1},{3,2},{4,3},{5,4},{6,5},{7,6},{8,7},{9,8},{10,9},{11,1... | collective-permute-start | bytes 1572872 | tf_op jit(solution)/shard_map/ppermute | solution.py:171
  8.4 14.4 %collective-permute-start.1 = (f32[8,16384]{1,0:T(8,128)S(1)}, f32[8,16384]{1,0:T(8,128)S(1)}, u32[]{:S(2)}, u32[]{:S(2)}) collective-permute-start(f32[8,16384]{1,0:T(8,128)S(1)} %maximum_maximum_fusion.refs_2_), channel_id=1, source_target_pairs={{0,1},{1,2},{2,3},{3,4},{4,5},{5,6},{6,7},{7,8},{8,9},{9,10},{10,1... | collective-permute-start | bytes 1572872 | tf_op jit(solution)/shard_map/ppermute | solution.py:171
  11.1 20.5 %collective-permute-start = (f32[8,16384]{1,0:T(8,128)S(1)}, f32[8,16384]{1,0:T(8,128)S(1)}, u32[]{:S(2)}, u32[]{:S(2)}) collective-permute-start(f32[8,16384]{1,0:T(8,128)S(1)} %maximum_maximum_fusion.refs_2_), channel_id=1, source_target_pairs={{0,2},{1,3},{2,4},{3,5},{4,6},{5,7},{6,8},{7,9},{8,10},{9,11},{10,... | collective-permute-start | bytes 1572872 | tf_op jit(solution)/shard_map/ppermute | solution.py:171
  13.7 0.7 copy-start
  13.7 0.7 copy-start.1
  108.0 10.9 %collective-permute-start.4 = (f32[3,16384]{1,0:T(4,128)S(1)}, f32[3,16384]{1,0:T(4,128)S(1)}, u32[]{:S(2)}, u32[]{:S(2)}) collective-permute-start(f32[3,16384]{1,0:T(4,128)S(1)} %get-tuple-element.11), channel_id=1, source_target_pairs={{2,0},{3,1},{4,2},{5,3},{6,4},{7,5},{8,6},{9,7},{10,8},{11,9},{12,... | collective-permute-start | bytes 589832 | tf_op jit(solution)/shard_map/ppermute | solution.py:171
  110.0 9.0 %collective-permute-start.5 = (f32[3,16384]{1,0:T(4,128)S(1)}, f32[3,16384]{1,0:T(4,128)S(1)}, u32[]{:S(2)}, u32[]{:S(2)}) collective-permute-start(f32[3,16384]{1,0:T(4,128)S(1)} %get-tuple-element.12), channel_id=1, source_target_pairs={{1,0},{2,1},{3,2},{4,3},{5,4},{6,5},{7,6},{8,7},{9,8},{10,9},{11,1... | collective-permute-start | bytes 589832 | tf_op jit(solution)/shard_map/ppermute | solution.py:171
  111.9 7.0 %collective-permute-start.6 = (f32[3,16384]{1,0:T(4,128)S(1)}, f32[3,16384]{1,0:T(4,128)S(1)}, u32[]{:S(2)}, u32[]{:S(2)}) collective-permute-start(f32[3,16384]{1,0:T(4,128)S(1)} %get-tuple-element.13), channel_id=1, source_target_pairs={{0,1},{1,2},{2,3},{3,4},{4,5},{5,6},{6,7},{7,8},{8,9},{9,10},{10,1... | collective-permute-start | bytes 589832 | tf_op jit(solution)/shard_map/ppermute | solution.py:171
  115.5 11.3 %collective-permute-start.7 = (f32[3,16384]{1,0:T(4,128)S(1)}, f32[3,16384]{1,0:T(4,128)S(1)}, u32[]{:S(2)}, u32[]{:S(2)}) collective-permute-start(f32[3,16384]{1,0:T(4,128)S(1)} %get-tuple-element.14), channel_id=1, source_target_pairs={{0,2},{1,3},{2,4},{3,5},{4,6},{5,7},{6,8},{7,9},{8,10},{9,11},{10,... | collective-permute-start | bytes 589832 | tf_op jit(solution)/shard_map/ppermute | solution.py:171

commit v2 on v1

--- a/solution.py
+++ b/solution.py
@@ -164,26 +164,134 @@
     )(first, second, count, *geos)
 
 
-def shifted(value, axis, by):
-    size = 1
-    for a in axis:
-        size *= lax.axis_size(a)
-    return lax.ppermute(value, axis, [(i, i + by) for i in range(size) if 0 <= i + by < size])
+MESH = pl.DeviceIdType.MESH
+
+
+def place(flat):
+    inner = lax.axis_size("gy")
+    total = lax.axis_size("gx") * inner
+    flat = (flat + total) % total
+    return (flat // inner, flat % inner)
+
+
+def greet(devices):
+    barrier = pltpu.get_barrier_semaphore()
+    for d in devices:
+        pl.semaphore_signal(barrier, inc=1, device_id=d, device_id_type=MESH)
+    pl.semaphore_wait(barrier, len(devices))
+
+
+def gather(geometry, rows, chunks):
+    faces = geometry.shape[1]
+    part = faces // chunks
+
+    def kernel(own, low, far, sib, high, send, recv):
+        me = lax.axis_index("gx") * lax.axis_size("gy") + lax.axis_index("gy")
+        odd = me % 2
+        up, down, other = place(me + 2), place(me - 2), place(me + 1 - 2 * odd)
+        greet((up, down, other))
+
+        def move(kind, i, src, dst, device):
+            sl = (pl.ds(0, rows), pl.ds(i * part, part))
+            return pltpu.make_async_remote_copy(
+                src_ref=src.at[sl],
+                dst_ref=dst.at[sl],
+                send_sem=send.at[kind, i],
+                recv_sem=recv.at[kind, i],
+                device_id=device,
+                device_id_type=MESH,
+            )
+
+        for i in range(chunks):
+            move(0, i, own, low, up).start()
+            move(1, i, own, high, down).start()
+        for i in range(chunks):
+            move(2, i, own, sib, other).start()
+        for i in range(chunks):
+            move(0, i, own, low, up).wait_recv()
+            move(1, i, own, high, down).wait_recv()
+
+            @pl.when(odd == 0)
+            def _():
+                move(3, i, high, far, other).start()
+
+            @pl.when(odd == 1)
+            def _():
+                move(3, i, low, far, other).start()
+
+        for i in range(chunks):
+            move(2, i, own, sib, other).wait_recv()
+            move(3, i, own, far, other).wait_recv()
+        for i in range(chunks):
+            move(0, i, own, low, up).wait_send()
+            move(1, i, own, high, down).wait_send()
+            move(2, i, own, sib, other).wait_send()
+            move(3, i, own, far, other).wait_send()
+
+    return pl.pallas_call(
+        kernel,
+        out_shape=[jax.ShapeDtypeStruct((8, faces), F32)] * 4,
+        in_specs=[pl.BlockSpec(memory_space=pl.ANY)],
+        out_specs=[pl.BlockSpec(memory_space=pl.ANY)] * 4,
+        scratch_shapes=[pltpu.SemaphoreType.DMA((4, chunks)), pltpu.SemaphoreType.DMA((4, chunks))],
+        compiler_params=pltpu.CompilerParams(collective_id=0, has_side_effects=True),
+    )(geometry)
+
+
+def give_back(own, low, far, sib, high):
+    faces = own.shape[1]
+
+    def kernel(own, low, far, sib, high, out, box, send, recv):
+        me = lax.axis_index("gx") * lax.axis_size("gy") + lax.axis_index("gy")
+        odd = me % 2
+        targets = (place(me - 2), place(me - 1 + 2 * odd), place(me + 1 - 2 * odd), place(me + 2))
+        greet(targets)
+        copies = [
+            pltpu.make_async_remote_copy(
+                src_ref=src,
+                dst_ref=box.at[k],
+                send_sem=send.at[k],
+                recv_sem=recv.at[k],
+                device_id=device,
+                device_id_type=MESH,
+            )
+            for k, (src, device) in enumerate(zip((low, far, sib, high), targets, strict=True))
+        ]
+        for k in (0, 3, 1, 2):
+            copies[k].start()
+        total = own[...]
+        for k in (2, 1, 0, 3):
+            copies[k].wait_recv()
+        out[...] = total + ((box[0] + box[3]) + (box[1] + box[2]))
+        for c in copies:
+            c.wait_send()
+
+    return pl.pallas_call(
+        kernel,
+        out_shape=jax.ShapeDtypeStruct((3, faces), F32),
+        in_specs=[pl.BlockSpec(memory_space=pltpu.VMEM)] * 5,
+        out_specs=pl.BlockSpec(memory_space=pltpu.VMEM),
+        scratch_shapes=[
+            pltpu.VMEM((4, 3, faces), F32),
+            pltpu.SemaphoreType.DMA((4,)),
+            pltpu.SemaphoreType.DMA((4,)),
+        ],
+        compiler_params=pltpu.CompilerParams(collective_id=1, has_side_effects=True),
+    )(own, low, far, sib, high)
 
 
 def body(positions, normals, areas, pair_first, pair_second, pair_count):
     faces = areas.shape[0]
     clusters = faces // C
-    axis = ("gx", "gy")
+    me = lax.axis_index(("gx", "gy"))
     geometry = jnp.concatenate([positions, normals, areas[None, :], jnp.zeros((1, faces), F32)], axis=0)
-    geos = [geometry if k == 0 else shifted(geometry, axis, -k) for k in range(-REACH, REACH + 1)]
-    base = (lax.axis_index(axis) - REACH) * clusters
-    outs = near_field(pair_first - base, pair_second - base, pair_count, geos)
-    owned = outs[REACH]
-    for k in range(-REACH, REACH + 1):
-        if k != 0:
-            owned = owned + shifted(outs[k + REACH], axis, k)
-    return owned
+    low, far, sib, high = gather(geometry, 8, 4)
+    first = pair_first - (me - REACH) * clusters
+    reach = pair_second // clusters - me
+    slot = REACH + jnp.where(jnp.abs(reach) == 1, reach * (1 - 2 * (me % 2)), reach)
+    second = slot * clusters + pair_second % clusters
+    outs = near_field(first, second, pair_count, [low, far, geometry, sib, high])
+    return give_back(outs[2], outs[0], outs[1], outs[3], outs[4])
 
 
 def solution(mesh):

time: 128 us -> 127 us (level)
  the two profiles are of different devices: /device:TPU:113 before, /device:TPU:10 now
where the time goes in v2:
time: 127 us
  Pallas kernels  114 us (90%)
  local copies, waits for them, and re-layouts  9.48 us (7%)
  other arithmetic  2.05 us (2%)
    pallas_call x1, Pallas kernels, give_back(): pl.pallas_call(kernel, out_shape=jax.ShapeDtypeStruct((3, faces), F32), i...  73.1 us
    pallas_call x1, Pallas kernels, near_field(): pl.pallas_call(kernel, out_shape=[jax.ShapeDtypeStruct((3, faces), F32)]...  21.1 us
    pallas_call x1, Pallas kernels, gather(): pl.pallas_call(kernel, out_shape=[jax.ShapeDtypeStruct((8, faces), F32)]...  20.2 us
    unnamed x25, local copies, waits for them, and re-layouts  9.41 us

profile of v2, /device:TPU:10, one launch (start us, length us, event | category | flops | bytes accessed | tf_op | source)
XLA Modules:
  0.0 126.7 jit_solution(4801956074516642224)
XLA Ops:
  0.0 0.0 copy-start.10
  0.0 0.0 copy-start.11
  0.7 0.0 copy-done.10
  0.7 0.0 copy-done.11
  0.7 0.1 pad.3.clone
  0.8 2.0 %maximum_maximum_fusion.own.refs_2_ = f32[8,16384]{1,0:T(8,128)} fusion(f32[1,16384]{1,0:T(1,128)} %bitcast.2, f32[3,16384]{1,0:T(4,128)} %param.7, f32[3,16384]{1,0:T(4,128)} %param.6, f32[8]{0:T(128)S(1)} %pad.3.clone), kind=kLoop, calls=%fused_computation | loop fusion | flops 393216 | bytes 983072 | tf_op jit(solution)/shard_map/concatenate | solution.py:287
  2.8 20.2 %shard_map.64 = (f32[8,16384]{1,0:T(8,128)}, f32[8,16384]{1,0:T(8,128)}, f32[8,16384]{1,0:T(8,128)}, f32[8,16384]{1,0:T(8,128)}) custom-call(f32[8,16384]{1,0:T(8,128)} %maximum_maximum_fusion.own.refs_2_), custom_call_target="tpu_custom_call" | custom-call | tf_op jit(solution)/shard_map/pallas_call | solution.py:231
  23.1 0.0 copy-done
  23.1 0.0 copy-start.1
  23.1 1.0 copy-done.1
  24.1 0.0 copy-start.2
  24.1 1.0 copy-done.2
  25.2 0.0 copy-start.3
  25.2 1.0 copy-done.3
  26.2 1.0 copy-done.4
  27.2 21.1 %shard_map.65 = (f32[3,16384]{1,0:T(4,128)S(1)}, f32[3,16384]{1,0:T(4,128)S(1)}, f32[3,16384]{1,0:T(4,128)S(1)}, f32[3,16384]{1,0:T(4,128)S(1)}, f32[3,16384]{1,0:T(4,128)S(1)}) custom-call(s32[128]{0:T(128)S(1)} %get-tuple-element.24.first, s32[128]{0:T(128)S(1)} %get-tuple-element.23.second, s32[1]{0:T(128)S(6)} %copy.8.count, f32[8,16384]{1,0:T(8,128)S(1)} %copy-done.1, ...), custom_call_target="tpu_custom_call" | custom-call | tf_op jit(solution)/shard_map/pallas_call | solution.py:157
  48.4 0.0 copy-start.5
  48.4 0.7 copy-done.5
  49.1 0.7 copy-done.6
  49.8 0.7 copy-done.7
  50.5 0.7 copy-done.8
  51.2 0.7 copy-done.9
  51.9 73.1 %shard_map.66 = f32[3,16384]{1,0:T(4,128)} custom-call(f32[3,16384]{1,0:T(4,128)} %copy-done.7, f32[3,16384]{1,0:T(4,128)} %copy-done.5, f32[3,16384]{1,0:T(4,128)} %copy-done.6, f32[3,16384]{1,0:T(4,128)} %copy-done.8, f32[3,16384]{1,0:T(4,128)} %copy-done.9), custom_call_target="tpu_custom_call" | custom-call | tf_op jit(solution)/shard_map/pallas_call | solution.py:269
  125.0 1.7 %copy.9 = f32[3,16384]{1,0:T(4,128)} copy(f32[3,16384]{1,0:T(4,128)} %shard_map.66) | data formatting | bytes 393216
  (7 shorter events, 0.0 us)
Async XLA Ops:
  0.0 0.7 copy-start.10
  0.0 0.7 copy-start.11
  2.8 20.2 %copy-start = (f32[8,16384]{1,0:T(8,128)S(1)}, f32[8,16384]{1,0:T(8,128)}, u32[]{:S(2)}) copy-start(f32[8,16384]{1,0:T(8,128)} %maximum_maximum_fusion.own.refs_2_) | copy-start | bytes 1572868
  23.1 1.0 copy-start.1
  24.1 1.0 copy-start.2
  25.2 1.0 copy-start.3
  26.2 1.0 copy-start.4
  48.4 0.7 copy-start.5
  49.1 0.7 copy-start.6
  49.8 0.7 copy-start.7
  50.5 0.7 copy-start.8
  51.2 0.7 copy-start.9

commit v3 on v2

v3 whole, which is shorter than its diff:
```python
import jax
import jax.numpy as jnp
from jax import lax
from jax.experimental import pallas as pl
from jax.experimental.pallas import tpu as pltpu
from jax.sharding import PartitionSpec as P

C = 256
REACH = 2
F32 = jnp.float32
BF = jnp.bfloat16
MESH = pl.DeviceIdType.MESH
VMEM_LIMIT = 60 * 2**20


def split3(t):
    a = t.astype(BF).astype(F32)
    r = t - a
    b = r.astype(BF).astype(F32)
    return a, b, r - b


def split2(t):
    a = t.astype(BF).astype(F32)
    return a, t - a


def wide(v):
    return jnp.broadcast_to(v, (8, C))


def row_index():
    return lax.broadcasted_iota(jnp.int32, (8, C), 0)


def prep(f, g, lhs_ref, rhs_ref, w_ref, keep_ref):
    row = row_index()
    isp = row < 3

    def at(k, v):
        return jnp.where(row == k, v, 0.0)

    af = wide(f[6:7, :])
    ag = wide(g[6:7, :])
    ctr = jnp.where(isp, wide(jnp.sum(f, axis=1, keepdims=True) * (1.0 / C)), 0.0)

    def parts(t):
        p = jnp.where(isp, t - ctr, 0.0)
        n = jnp.where(isp, pltpu.roll(t, 5, 0), 0.0)
        return p, n, wide(jnp.sum(p * p, axis=0, keepdims=True)), wide(jnp.sum(p * n, axis=0, keepdims=True))

    pf, nf, sf, cf = parts(f)
    pg, ng, sg, cg = parts(g)
    iaf = 1.0 / af
    iag = 1.0 / ag

    def left(t):
        u0, u1, u2 = split3(t)
        return jnp.concatenate([u0, u0, u0, u1, u1, u2], axis=0).T.astype(BF)

    def right(t):
        u0, u1, u2 = split3(t)
        return jnp.concatenate([u0, u1, u2, u0, u1, u0], axis=0).astype(BF)

    lhs_ref[0] = left(pf + at(3, sf + 1.0) + at(4, 1.0))
    lhs_ref[1] = left(af * (nf + at(3, cf) + pltpu.roll(pf, 4, 0) + at(7, 1.0)))
    rhs_ref[0] = right(-2.0 * pg + at(3, 1.0) + at(4, sg))
    rhs_ref[1] = right(ag * (at(3, 1.0) - pg))
    rhs_ref[2] = right(ag * (pltpu.roll(ng, 4, 0) - at(7, cg)))
    sums = (2.0 * nf, iaf * (at(6, 6.0) - 6.0 * pltpu.roll(pf, 3, 0)), iag * (6.0 * pg - at(3, 6.0)))
    for j, v in enumerate(sums):
        w_ref[j] = jnp.concatenate(split2(v), axis=0).astype(BF)
    for i, v in enumerate((nf, pf, iaf, ng, pg, iag)):
        keep_ref[i] = v


def terms(base, rows, sub, n, cs, lhs_ref, rhs_ref, l_ref, x_ref):
    def half(v):
        return v[:, :128] + v[:, 128:]

    big = slice(base, base + rows)
    left = lhs_ref[1, big, :]
    all_r2 = jnp.dot(lhs_ref[0, big, :], rhs_ref[0], preferred_element_type=F32)
    all_sf = jnp.dot(left, rhs_ref[1], preferred_element_type=F32)
    all_sg = jnp.dot(left, rhs_ref[2], preferred_element_type=F32)
    for s in range(0, rows, sub):
        sl = slice(base + s, base + s + sub)
        q = slice(s, s + sub)
        inv = 1.0 / all_r2[q]
        sf = all_sf[q]
        sg = all_sg[q]
        inv3 = inv * inv * inv
        lf = inv3 * sf
        lg = inv3 * sg
        rad = inv * (lf * sf + lg * sg)
        for j, v in ((0, lf), (2, rad)):
            h = v.astype(BF)
            l_ref[j, sl, :] = h
            l_ref[j + 1, sl, :] = (v - h.astype(F32)).astype(BF)
        for t in range(0, sub, 8):
            o = slice(t, t + 8)
            so = slice(base + s + t, base + s + t + 8)
            cs = cs + lg[o]
            x_ref[3, so, :] = half(lf[o])
            for k in range(3):
                x_ref[k, so, :] = half(lg[o] * n[k])
    return cs


def along(w, tile):
    return lax.dot_general(w, tile, (((1,), (0,)), ((), ())), preferred_element_type=F32)


def across(w, tile):
    return lax.dot_general(w, tile, (((1,), (1,)), ((), ())), preferred_element_type=F32)


def stage(h, now, before, ws, ks, load, save, rows=64, sub=16):
    lhs, rhs, w, keep, tiles, x, csr = now
    w_b, keep_b, tiles_b, x_b, csr_b = before[2:]
    ws[...] = w_b[...]
    ks[...] = keep_b[...]
    normal = [wide(keep[3, k : k + 1, :]) for k in range(3)]
    cs = jnp.zeros((8, C), F32)
    xs = [[None, None] for _ in range(4)]
    col = []
    rsum = []
    count = C // rows
    for c in range(count):
        cs = terms(c * rows, rows, sub, normal, cs, lhs, rhs, tiles, x)
        for e in range(c * 8 // count, (c + 1) * 8 // count):
            k, s = e // 2, e % 2
            xs[k][s] = jnp.sum(x_b[k, s * 128 : (s + 1) * 128, :].T, axis=0, keepdims=True)
            if e < 4:
                col.append(along(ws[e // 2], tiles_b[e]))
            elif e < 6:
                rsum.append(across(ws[2], tiles_b[e - 2]))
        if c == count // 2 - 1:
            prep(*load(h + 1), *before[:4])
    csr_old = csr_b[...]
    csr[...] = cs
    row = row_index()
    ct = (col[0] + col[1]) + (col[2] + col[3])
    rt = rsum[0] + rsum[1]
    ct = ct[0:8] + ct[8:16]
    rt = rt[0:8] + rt[8:16]
    nf, pf, iaf, ng, pg, iag = (ks[i] for i in range(6))
    xv = [wide(jnp.concatenate(v, axis=1)) for v in xs]
    lean = jnp.where(row == 0, xv[0], jnp.where(row == 1, xv[1], xv[2]))
    gf = 2.0 * (nf * xv[3] + lean) + iaf * (rt + pf * wide(rt[3:4]))
    csum = wide(jnp.sum(csr_old, axis=0, keepdims=True))
    gg = -(ct + ng * (2.0 * csum) + iag * (pltpu.roll(ct, 5, 0) + pg * wide(ct[6:7])))
    save(h - 1, gf, gg)


STAGE = [
    pltpu.VMEM((2, C, 48), BF),
    pltpu.VMEM((3, 48, C), BF),
    pltpu.VMEM((3, 16, C), BF),
    pltpu.VMEM((6, 8, C), F32),
    pltpu.VMEM((4, C, C), BF),
    pltpu.VMEM((4, C, 128), F32),
    pltpu.VMEM((8, C), F32),
]
KEPT = [pltpu.VMEM((3, 16, C), BF), pltpu.VMEM((6, 8, C), F32)]


def lanes(c):
    return pl.ds(pl.multiple_of(c * C, C), C)


def near_field(first, second, count, geos):
    nwin = len(geos)
    faces = geos[0].shape[1]
    slots = first.shape[0]

    def kernel(first, second, count, *refs):
        geo = refs[:nwin]
        outs = refs[nwin : 2 * nwin]
        win, acc = refs[2 * nwin : 2 * nwin + 2]
        even = refs[2 * nwin + 2 : 2 * nwin + 9]
        odd = refs[2 * nwin + 9 : 2 * nwin + 16]
        ws, ks, sem = refs[2 * nwin + 16 :]
        copies = [
            pltpu.make_async_copy(geo[k], win.at[:, pl.ds(k * faces, faces)], sem.at[k]) for k in range(nwin)
        ]
        for c in copies:
            c.start()
        acc[...] = jnp.zeros_like(acc)
        for c in copies:
            c.wait()
        n = count[0]

        def load(h):
            q = jnp.minimum(h, slots - 1)
            return win[:, lanes(first[q])], win[:, lanes(second[q])]

        def save(h, gf, gg):
            live = (h >= 0) & (h < n)
            q = jnp.clip(h, 0, slots - 1)
            fi = lanes(first[q])
            si = lanes(second[q])
            acc[:, fi] += jnp.where(live, gf, 0.0)
            acc[:, si] += jnp.where(live, gg, 0.0)

        prep(*load(0), *even[:4])

        def step(i, carry):
            stage(2 * i, even, odd, ws, ks, load, save)
            stage(2 * i + 1, odd, even, ws, ks, load, save)
            return carry

        lax.fori_loop(0, (n + 2) // 2, step, 0)
        for k in range(nwin):
            outs[k][...] = acc[0:3, k * faces : (k + 1) * faces]

    return pl.pallas_call(
        kernel,
        out_shape=[jax.ShapeDtypeStruct((3, faces), F32)] * nwin,
        in_specs=[pl.BlockSpec(memory_space=pltpu.SMEM)] * 3 + [pl.BlockSpec(memory_space=pl.ANY)] * nwin,
        out_specs=[pl.BlockSpec(memory_space=pltpu.VMEM)] * nwin,
        scratch_shapes=[pltpu.VMEM((8, nwin * faces), F32)] * 2
        + STAGE
        + STAGE
        + KEPT
        + [pltpu.SemaphoreType.DMA((nwin,))],
        compiler_params=pltpu.CompilerParams(vmem_limit_bytes=VMEM_LIMIT),
    )(first, second, count, *geos)


def place(flat):
    inner = lax.axis_size("gy")
    total = lax.axis_size("gx") * inner
    flat = (flat + total) % total
    return (flat // inner, flat % inner)


def greet(devices):
    barrier = pltpu.get_barrier_semaphore()
    for d in devices:
        pl.semaphore_signal(barrier, inc=1, device_id=d, device_id_type=MESH)
    pl.semaphore_wait(barrier, len(devices))


def gather(geometry, rows, chunks):
    faces = geometry.shape[1]
    part = faces // chunks

    def kernel(own, low, far, sib, high, send, recv):
        me = lax.axis_index("gx") * lax.axis_size("gy") + lax.axis_index("gy")
        odd = me % 2
        up, down, other = place(me + 2), place(me - 2), place(me + 1 - 2 * odd)
        greet((up, down, other))

        def move(kind, i, src, dst, device):
            sl = (pl.ds(0, rows), pl.ds(i * part, part))
            return pltpu.make_async_remote_copy(
                src_ref=src.at[sl],
                dst_ref=dst.at[sl],
                send_sem=send.at[kind, i],
                recv_sem=recv.at[kind, i],
                device_id=device,
                device_id_type=MESH,
            )

        for i in range(chunks):
            move(0, i, own, low, up).start()
            move(1, i, own, high, down).start()
        for i in range(chunks):
            move(2, i, own, sib, other).start()
        for i in range(chunks):
            move(0, i, own, low, up).wait_recv()
            move(1, i, own, high, down).wait_recv()

            @pl.when(odd == 0)
            def _():
                move(3, i, high, far, other).start()

            @pl.when(odd == 1)
            def _():
                move(3, i, low, far, other).start()

        for i in range(chunks):
            move(2, i, own, sib, other).wait_recv()
            move(3, i, own, far, other).wait_recv()
        for i in range(chunks):
            move(0, i, own, low, up).wait_send()
            move(1, i, own, high, down).wait_send()
            move(2, i, own, sib, other).wait_send()
            move(3, i, own, far, other).wait_send()

    return pl.pallas_call(
        kernel,
        out_shape=[jax.ShapeDtypeStruct((8, faces), F32)] * 4,
        in_specs=[pl.BlockSpec(memory_space=pl.ANY)],
        out_specs=[pl.BlockSpec(memory_space=pl.ANY)] * 4,
        scratch_shapes=[pltpu.SemaphoreType.DMA((4, chunks)), pltpu.SemaphoreType.DMA((4, chunks))],
        compiler_params=pltpu.CompilerParams(
            collective_id=0, has_side_effects=True, vmem_limit_bytes=VMEM_LIMIT
        ),
    )(geometry)


def give_back(low, far, sib, high):
    faces = low.shape[1]

    def kernel(low, far, sib, high, *refs):
        boxes = refs[:4]
        send, recv = refs[4:]
        me = lax.axis_index("gx") * lax.axis_size("gy") + lax.axis_index("gy")
        odd = me % 2
        targets = (place(me - 2), place(me - 1 + 2 * odd), place(me + 1 - 2 * odd), place(me + 2))
        greet(targets)
        copies = [
            pltpu.make_async_remote_copy(
                src_ref=src,
                dst_ref=boxes[k],
                send_sem=send.at[k],
                recv_sem=recv.at[k],
                device_id=device,
                device_id_type=MESH,
            )
            for k, (src, device) in enumerate(zip((low, far, sib, high), targets, strict=True))
        ]
        for k in (0, 3, 1, 2):
            copies[k].start()
        for c in copies:
            c.wait()

    return pl.pallas_call(
        kernel,
        out_shape=[jax.ShapeDtypeStruct((3, faces), F32)] * 4,
        in_specs=[pl.BlockSpec(memory_space=pl.ANY)] * 4,
        out_specs=[pl.BlockSpec(memory_space=pl.ANY)] * 4,
        scratch_shapes=[pltpu.SemaphoreType.DMA((4,)), pltpu.SemaphoreType.DMA((4,))],
        compiler_params=pltpu.CompilerParams(
            collective_id=1, has_side_effects=True, vmem_limit_bytes=VMEM_LIMIT
        ),
    )(low, far, sib, high)


def body(positions, normals, areas, pair_first, pair_second, pair_count):
    faces = areas.shape[0]
    clusters = faces // C
    me = lax.axis_index(("gx", "gy"))
    geometry = jnp.concatenate([positions, normals, areas[None, :], jnp.zeros((1, faces), F32)], axis=0)
    low, far, sib, high = gather(geometry, 7, 4)
    first = pair_first - (me - REACH) * clusters
    reach = pair_second // clusters - me
    slot = REACH + jnp.where(jnp.abs(reach) == 1, reach * (1 - 2 * (me % 2)), reach)
    second = slot * clusters + pair_second % clusters
    outs = near_field(first, second, pair_count, [low, far, geometry, sib, high])
    boxes = give_back(outs[0], outs[1], outs[3], outs[4])
    return outs[2] + ((boxes[0] + boxes[3]) + (boxes[1] + boxes[2]))


def solution(mesh):
    flat = P(("gx", "gy"))
    deep = P(None, ("gx", "gy"))
    return jax.shard_map(
        body, mesh=mesh, in_specs=(deep, deep, flat, flat, flat, flat), out_specs=deep, check_vma=False
    )
```

time: 127 us -> 95.9 us (0.76)
  the two profiles are of different devices: /device:TPU:10 before, /device:TPU:16 now
where the time goes in v3:
time: 95.9 us
  Pallas kernels  90.4 us (94%)
  other arithmetic  4.63 us (5%)
    pallas_call x1, Pallas kernels, near_field(): pl.pallas_call(kernel, out_shape=[jax.ShapeDtypeStruct((3, faces), F32)]...  55.1 us
    pallas_call x1, Pallas kernels, gather(): pl.pallas_call(kernel, out_shape=[jax.ShapeDtypeStruct((8, faces), F32)]...  19.2 us
    pallas_call x1, Pallas kernels, give_back(): pl.pallas_call(kernel, out_shape=[jax.ShapeDtypeStruct((3, faces), F32)]...  16.2 us
    concatenate x1, other arithmetic, body(): jnp.concatenate([positions, normals, areas[None, :], jnp.zeros((1, faces)...  2.03 us
    add x1, other arithmetic, body(): return outs[2] + (boxes[0] + boxes[3] + (boxes[1] + boxes[2]))  2.03 us

profile of v3, /device:TPU:16, one launch (start us, length us, event | category | flops | bytes accessed | tf_op | source)
XLA Modules:
  0.0 95.9 jit_solution(9214889752617496938)
XLA Ops:
  0.0 0.0 copy-start.1
  0.0 0.0 copy-start.2
  0.7 0.0 copy-done.1
  0.7 0.0 copy-done.2
  0.7 0.6 fusion
  1.3 0.1 pad.3.clone
  1.3 2.0 %maximum_maximum_fusion.own.refs_2_ = f32[8,16384]{1,0:T(8,128)} fusion(f32[1,16384]{1,0:T(1,128)} %bitcast.2, f32[3,16384]{1,0:T(4,128)} %param.7, f32[3,16384]{1,0:T(4,128)} %param.6, f32[8]{0:T(128)S(1)} %pad.3.clone), kind=kLoop, calls=%fused_computation | loop fusion | flops 393216 | bytes 983072 | tf_op jit(solution)/shard_map/concatenate | solution.py:346
  3.4 19.2 %shard_map.64 = (f32[8,16384]{1,0:T(8,128)}, f32[8,16384]{1,0:T(8,128)}, f32[8,16384]{1,0:T(8,128)}, f32[8,16384]{1,0:T(8,128)}) custom-call(f32[8,16384]{1,0:T(8,128)} %maximum_maximum_fusion.own.refs_2_), custom_call_target="tpu_custom_call" | custom-call | tf_op jit(solution)/shard_map/pallas_call | solution.py:292
  22.6 55.1 %shard_map.65 = (f32[3,16384]{1,0:T(4,128)}, f32[3,16384]{1,0:T(4,128)}, f32[3,16384]{1,0:T(4,128)}, f32[3,16384]{1,0:T(4,128)}, f32[3,16384]{1,0:T(4,128)}) custom-call(s32[128]{0:T(128)} %get-tuple-element.32.first, s32[128]{0:T(128)} %get-tuple-element.31.second, s32[1]{0:T(128)S(6)} %copy.7.count, f32[8,16384]{1,0:T(8,128)} %get-tuple-element.18.refs_0_, ...), custom_call_target="tpu_custom_call" | custom-call | tf_op jit(solution)/shard_map/pallas_call | solution.py:217
  77.7 0.0 copy-start
  77.7 16.2 %shard_map.66 = (f32[3,16384]{1,0:T(4,128)}, f32[3,16384]{1,0:T(4,128)}, f32[3,16384]{1,0:T(4,128)}, f32[3,16384]{1,0:T(4,128)}) custom-call(f32[3,16384]{1,0:T(4,128)} %get-tuple-element.23.low, f32[3,16384]{1,0:T(4,128)} %get-tuple-element.24.far, f32[3,16384]{1,0:T(4,128)} %get-tuple-element.25.sib, f32[3,16384]{1,0:T(4,128)} %get-tuple-element.26.high), custom_call_target="tpu_custom_call" | custom-call | tf_op jit(solution)/shard_map/pallas_call | solution.py:330
  93.8 0.0 copy-done
  93.9 2.0 %add_add_fusion = f32[3,16384]{1,0:T(4,128)} fusion(f32[3,16384]{1,0:T(4,128)S(1)} %copy-done, f32[3,16384]{1,0:T(4,128)} %get-tuple-element.29, f32[3,16384]{1,0:T(4,128)} %get-tuple-element.30, f32[3,16384]{1,0:T(4,128)} %get-tuple-element.27, f32[3,16384]{1,0:T(4,128)} %get-tuple-element.28), kind=kLoop, calls=%fused_computation.1 | loop fusion | flops 196608 | bytes 1179648 | tf_op jit(solution)/shard_map/add | solution.py:354
Async XLA Ops:
  0.0 0.7 copy-start.1
  0.0 0.7 copy-start.2
  77.7 16.2 %copy-start = (f32[3,16384]{1,0:T(4,128)S(1)}, f32[3,16384]{1,0:T(4,128)}, u32[]{:S(2)}) copy-start(f32[3,16384]{1,0:T(4,128)} %get-tuple-element.22) | copy-start | bytes 589828

commit v4 on v3

--- a/solution.py
+++ b/solution.py
@@ -11,6 +11,9 @@
 BF = jnp.bfloat16
 MESH = pl.DeviceIdType.MESH
 VMEM_LIMIT = 60 * 2**20
+EARLY = 31
+LATE = 31
+ROW = 128
 
 
 def split3(t):
@@ -169,65 +172,6 @@
     return pl.ds(pl.multiple_of(c * C, C), C)
 
 
-def near_field(first, second, count, geos):
-    nwin = len(geos)
-    faces = geos[0].shape[1]
-    slots = first.shape[0]
-
-    def kernel(first, second, count, *refs):
-        geo = refs[:nwin]
-        outs = refs[nwin : 2 * nwin]
-        win, acc = refs[2 * nwin : 2 * nwin + 2]
-        even = refs[2 * nwin + 2 : 2 * nwin + 9]
-        odd = refs[2 * nwin + 9 : 2 * nwin + 16]
-        ws, ks, sem = refs[2 * nwin + 16 :]
-        copies = [
-            pltpu.make_async_copy(geo[k], win.at[:, pl.ds(k * faces, faces)], sem.at[k]) for k in range(nwin)
-        ]
-        for c in copies:
-            c.start()
-        acc[...] = jnp.zeros_like(acc)
-        for c in copies:
-            c.wait()
-        n = count[0]
-
-        def load(h):
-            q = jnp.minimum(h, slots - 1)
-            return win[:, lanes(first[q])], win[:, lanes(second[q])]
-
-        def save(h, gf, gg):
-            live = (h >= 0) & (h < n)
-            q = jnp.clip(h, 0, slots - 1)
-            fi = lanes(first[q])
-            si = lanes(second[q])
-            acc[:, fi] += jnp.where(live, gf, 0.0)
-            acc[:, si] += jnp.where(live, gg, 0.0)
-
-        prep(*load(0), *even[:4])
-
-        def step(i, carry):
-            stage(2 * i, even, odd, ws, ks, load, save)
-            stage(2 * i + 1, odd, even, ws, ks, load, save)
-            return carry
-
-        lax.fori_loop(0, (n + 2) // 2, step, 0)
-        for k in range(nwin):
-            outs[k][...] = acc[0:3, k * faces : (k + 1) * faces]
-
-    return pl.pallas_call(
-        kernel,
-        out_shape=[jax.ShapeDtypeStruct((3, faces), F32)] * nwin,
-        in_specs=[pl.BlockSpec(memory_space=pltpu.SMEM)] * 3 + [pl.BlockSpec(memory_space=pl.ANY)] * nwin,
-        out_specs=[pl.BlockSpec(memory_space=pltpu.VMEM)] * nwin,
-        scratch_shapes=[pltpu.VMEM((8, nwin * faces), F32)] * 2
-        + STAGE
-        + STAGE
-        + KEPT
-        + [pltpu.SemaphoreType.DMA((nwin,))],
-        compiler_params=pltpu.CompilerParams(vmem_limit_bytes=VMEM_LIMIT),
-    )(first, second, count, *geos)
-
-
 def place(flat):
     inner = lax.axis_size("gy")
     total = lax.axis_size("gx") * inner
@@ -235,6 +179,10 @@
     return (flat // inner, flat % inner)
 
 
+def position():
+    return lax.axis_index("gx") * lax.axis_size("gy") + lax.axis_index("gy")
+
+
 def greet(devices):
     barrier = pltpu.get_barrier_semaphore()
     for d in devices:
@@ -242,18 +190,84 @@
     pl.semaphore_wait(barrier, len(devices))
 
 
-def gather(geometry, rows, chunks):
-    faces = geometry.shape[1]
-    part = faces // chunks
-
-    def kernel(own, low, far, sib, high, send, recv):
-        me = lax.axis_index("gx") * lax.axis_size("gy") + lax.axis_index("gy")
+def sort_out(positions, normals, areas, pair_first, pair_second, pair_count):
+    faces = positions.shape[1]
+    clusters = faces // C
+
+    def kernel(pos, nor, area, pf, ps, count, geometry, lists):
+        for c in range(clusters):
+            sl = slice(c * C, (c + 1) * C)
+            geometry[c, 0:3, :] = pos[:, sl]
+            geometry[c, 3:6, :] = nor[:, sl]
+            geometry[c, 6:7, :] = area[:, sl]
+            geometry[c, 7:8, :] = jnp.zeros((1, C), F32)
+        me = position()
+        odd = me % 2
+
+        def clear(i, carry):
+            for r in range(4):
+                lists[r * ROW + i] = 0
+            return carry
+
+        lax.fori_loop(0, EARLY + 1, clear, 0)
+        lists[4 * ROW] = 0
+        lists[5 * ROW] = 0
+
+        def step(j, carry):
+            n1, n3, n2 = carry
+            f = pf[j] - me * clusters
+            s = ps[j]
+            owner = s // clusters
+            local = s - owner * clusters
+            h = owner - me
+            beside = h == 1 - 2 * odd
+            inside = h == 0
+            late = inside & (n3 < LATE)
+            early = (beside | inside) & (n1 < EARLY) & jnp.logical_not(late)
+            rest = jnp.logical_not(late | early)
+            near = (h == 1) | (h == -1)
+            slot = REACH + jnp.where(near, h * (1 - 2 * odd), h)
+            base = jnp.where(late, 2 * ROW + n3, jnp.where(early, n1, 4 * ROW + n2))
+            lists[base] = jnp.where(rest, f + REACH * clusters, f)
+            lists[base + ROW] = jnp.where(rest, slot * clusters, jnp.where(beside, clusters, 0)) + local
+            return (
+                n1 + early.astype(jnp.int32),
+                n3 + late.astype(jnp.int32),
+                n2 + rest.astype(jnp.int32),
+            )
+
+        n1, n3, n2 = lax.fori_loop(0, count[0], step, (0, 0, 0))
+        lists[6 * ROW] = n1
+        lists[6 * ROW + 1] = n3
+        lists[6 * ROW + 2] = n2
+
+    vmem = pl.BlockSpec(memory_space=pltpu.VMEM)
+    smem = pl.BlockSpec(memory_space=pltpu.SMEM)
+    return pl.pallas_call(
+        kernel,
+        out_shape=[jax.ShapeDtypeStruct((clusters, 8, C), F32), jax.ShapeDtypeStruct((7 * ROW,), jnp.int32)],
+        in_specs=[vmem] * 3 + [smem] * 3,
+        out_specs=[vmem, smem],
+        compiler_params=pltpu.CompilerParams(vmem_limit_bytes=VMEM_LIMIT),
+    )(positions, normals, areas.reshape(1, faces), pair_first, pair_second, pair_count)
+
+
+def gather(geometry, lists, rows=7, chunks=4):
+    clusters = geometry.shape[0]
+    part = clusters // chunks
+
+    def kernel(own, lists, low, far, sib, high, made, seen, *refs):
+        even, odds = refs[:7], refs[7:14]
+        ws, ks, send, recv, fetch = refs[14:]
+        me = position()
         odd = me % 2
         up, down, other = place(me + 2), place(me - 2), place(me + 1 - 2 * odd)
+        mine = pltpu.make_async_copy(own, seen.at[pl.ds(0, clusters)], fetch.at[0])
+        mine.start()
         greet((up, down, other))
 
         def move(kind, i, src, dst, device):
-            sl = (pl.ds(0, rows), pl.ds(i * part, part))
+            sl = (pl.ds(i * part, part), pl.ds(0, rows))
             return pltpu.make_async_remote_copy(
                 src_ref=src.at[sl],
                 dst_ref=dst.at[sl],
@@ -266,9 +280,32 @@
         for i in range(chunks):
             move(0, i, own, low, up).start()
             move(1, i, own, high, down).start()
-        for i in range(chunks):
             move(2, i, own, sib, other).start()
         for i in range(chunks):
+            move(2, i, own, sib, other).wait_recv()
+        beside = pltpu.make_async_copy(sib, seen.at[pl.ds(clusters, clusters)], fetch.at[1])
+        beside.start()
+        mine.wait()
+        beside.wait()
+
+        def load(h):
+            q = jnp.minimum(h, EARLY)
+            return seen[lists[q]], seen[lists[ROW + q]]
+
+        def save(h, gf, gg):
+            made[h + 1, 0] = gf
+            made[h + 1, 1] = gg
+
+        prep(*load(0), *even[:4])
+
+        def step(i, carry):
+            stage(2 * i, even, odds, ws, ks, load, save)
+            stage(2 * i + 1, odds, even, ws, ks, load, save)
+            return carry
+
+        halves = (EARLY + 1) // 2
+        for i in range(chunks):
+            lax.fori_loop(i * halves // chunks, (i + 1) * halves // chunks, step, 0)
             move(0, i, own, low, up).wait_recv()
             move(1, i, own, high, down).wait_recv()
 
@@ -281,35 +318,113 @@
                 move(3, i, low, far, other).start()
 
         for i in range(chunks):
-            move(2, i, own, sib, other).wait_recv()
             move(3, i, own, far, other).wait_recv()
         for i in range(chunks):
-            move(0, i, own, low, up).wait_send()
-            move(1, i, own, high, down).wait_send()
-            move(2, i, own, sib, other).wait_send()
-            move(3, i, own, far, other).wait_send()
-
+            for kind in range(4):
+                move(kind, i, own, low, up).wait_send()
+
+    hbm = pl.BlockSpec(memory_space=pl.ANY)
     return pl.pallas_call(
         kernel,
-        out_shape=[jax.ShapeDtypeStruct((8, faces), F32)] * 4,
-        in_specs=[pl.BlockSpec(memory_space=pl.ANY)],
-        out_specs=[pl.BlockSpec(memory_space=pl.ANY)] * 4,
-        scratch_shapes=[pltpu.SemaphoreType.DMA((4, chunks)), pltpu.SemaphoreType.DMA((4, chunks))],
+        out_shape=[jax.ShapeDtypeStruct((clusters, 8, C), F32)] * 4
+        + [jax.ShapeDtypeStruct((EARLY + 1, 2, 8, C), F32)],
+        in_specs=[hbm, pl.BlockSpec(memory_space=pltpu.SMEM)],
+        out_specs=[hbm] * 4 + [pl.BlockSpec(memory_space=pltpu.VMEM)],
+        scratch_shapes=[pltpu.VMEM((2 * clusters, 8, C), F32)]
+        + STAGE
+        + STAGE
+        + KEPT
+        + [pltpu.SemaphoreType.DMA((4, chunks)), pltpu.SemaphoreType.DMA((4, chunks)), pltpu.SemaphoreType.DMA((2,))],
         compiler_params=pltpu.CompilerParams(
             collective_id=0, has_side_effects=True, vmem_limit_bytes=VMEM_LIMIT
         ),
-    )(geometry)
-
-
-def give_back(low, far, sib, high):
+    )(geometry, lists)
+
+
+def near_field(lists, geos, made, sib_slot):
+    nwin = len(geos)
+    clusters = geos[0].shape[0]
+    faces = clusters * C
+
+    def kernel(lists, made, *refs):
+        geo = refs[:nwin]
+        outs = refs[nwin : 2 * nwin]
+        win, acc, early = refs[2 * nwin : 2 * nwin + 3]
+        even = refs[2 * nwin + 3 : 2 * nwin + 10]
+        odd = refs[2 * nwin + 10 : 2 * nwin + 17]
+        ws, ks, sem = refs[2 * nwin + 17 :]
+        copies = [
+            pltpu.make_async_copy(geo[k], win.at[pl.ds(k * clusters, clusters)], sem.at[k]) for k in range(nwin)
+        ] + [pltpu.make_async_copy(made, early, sem.at[nwin])]
+        for c in copies:
+            c.start()
+        acc[...] = jnp.zeros_like(acc)
+        for c in copies:
+            c.wait()
+        n = lists[6 * ROW + 2]
+        last = jnp.maximum(n - 1, 0)
+
+        def load(h):
+            q = jnp.minimum(h, last)
+            return win[lists[4 * ROW + q]], win[lists[5 * ROW + q]]
+
+        def save(h, gf, gg):
+            live = (h >= 0) & (h < n)
+            q = jnp.clip(h, 0, last)
+            fi = lists[4 * ROW + q]
+            si = lists[5 * ROW + q]
+            acc[fi] += jnp.where(live, gf, 0.0)
+            acc[si] += jnp.where(live, gg, 0.0)
+
+        prep(*load(0), *even[:4])
+
+        def add(j, carry):
+            acc[lists[j] + sib_slot * clusters] += early[j + 1, 0]
+            acc[lists[ROW + j] + sib_slot * clusters] += early[j + 1, 1]
+            return carry
+
+        lax.fori_loop(0, lists[6 * ROW], add, 0)
+
+        def step(i, carry):
+            stage(2 * i, even, odd, ws, ks, load, save)
+            stage(2 * i + 1, odd, even, ws, ks, load, save)
+            return carry
+
+        lax.fori_loop(0, (n + 2) // 2, step, 0)
+        for k in range(nwin):
+            for c in range(clusters):
+                outs[k][:, c * C : (c + 1) * C] = acc[k * clusters + c, 0:3, :]
+
+    hbm = pl.BlockSpec(memory_space=pl.ANY)
+    return pl.pallas_call(
+        kernel,
+        out_shape=[jax.ShapeDtypeStruct((3, faces), F32)] * nwin,
+        in_specs=[pl.BlockSpec(memory_space=pltpu.SMEM)] + [hbm] * (nwin + 1),
+        out_specs=[pl.BlockSpec(memory_space=pltpu.VMEM)] * nwin,
+        scratch_shapes=[pltpu.VMEM((nwin * clusters, 8, C), F32)] * 2
+        + [pltpu.VMEM((EARLY + 1, 2, 8, C), F32)]
+        + STAGE
+        + STAGE
+        + KEPT
+        + [pltpu.SemaphoreType.DMA((nwin + 1,))],
+        compiler_params=pltpu.CompilerParams(vmem_limit_bytes=VMEM_LIMIT),
+    )(lists, made, *geos)
+
+
+def give_back(low, far, sib, high, geometry, lists):
     faces = low.shape[1]
-
-    def kernel(low, far, sib, high, *refs):
+    clusters = faces // C
+
+    def kernel(low, far, sib, high, own, lists, *refs):
         boxes = refs[:4]
-        send, recv = refs[4:]
-        me = lax.axis_index("gx") * lax.axis_size("gy") + lax.axis_index("gy")
+        made, seen = refs[4:6]
+        even, odds = refs[6:13], refs[13:20]
+        ws, ks, send, recv, fetch = refs[20:]
+        me = position()
         odd = me % 2
         targets = (place(me - 2), place(me - 1 + 2 * odd), place(me + 1 - 2 * odd), place(me + 2))
+        mine = pltpu.make_async_copy(own, seen, fetch.at[0])
+        mine.start()
         greet(targets)
         copies = [
             pltpu.make_async_remote_copy(
@@ -324,34 +439,74 @@
         ]
         for k in (0, 3, 1, 2):
             copies[k].start()
+        mine.wait()
+
+        def load(h):
+            q = jnp.minimum(h, LATE)
+            return seen[lists[2 * ROW + q]], seen[lists[3 * ROW + q]]
+
+        def save(h, gf, gg):
+            made[h + 1, 0] = gf
+            made[h + 1, 1] = gg
+
+        prep(*load(0), *even[:4])
+
+        def step(i, carry):
+            stage(2 * i, even, odds, ws, ks, load, save)
+            stage(2 * i + 1, odds, even, ws, ks, load, save)
+            return carry
+
+        lax.fori_loop(0, (LATE + 1) // 2, step, 0)
         for c in copies:
             c.wait()
 
+    hbm = pl.BlockSpec(memory_space=pl.ANY)
     return pl.pallas_call(
         kernel,
-        out_shape=[jax.ShapeDtypeStruct((3, faces), F32)] * 4,
-        in_specs=[pl.BlockSpec(memory_space=pl.ANY)] * 4,
-        out_specs=[pl.BlockSpec(memory_space=pl.ANY)] * 4,
-        scratch_shapes=[pltpu.SemaphoreType.DMA((4,)), pltpu.SemaphoreType.DMA((4,))],
+        out_shape=[jax.ShapeDtypeStruct((3, faces), F32)] * 4
+        + [jax.ShapeDtypeStruct((LATE + 1, 2, 8, C), F32)],
+        in_specs=[hbm] * 5 + [pl.BlockSpec(memory_space=pltpu.SMEM)],
+        out_specs=[hbm] * 4 + [pl.BlockSpec(memory_space=pltpu.VMEM)],
+        scratch_shapes=[pltpu.VMEM((clusters, 8, C), F32)]
+        + STAGE
+        + STAGE
+        + KEPT
+        + [pltpu.SemaphoreType.DMA((4,)), pltpu.SemaphoreType.DMA((4,)), pltpu.SemaphoreType.DMA((1,))],
         compiler_params=pltpu.CompilerParams(
             collective_id=1, has_side_effects=True, vmem_limit_bytes=VMEM_LIMIT
         ),
-    )(low, far, sib, high)
+    )(low, far, sib, high, geometry, lists)
+
+
+def finish(own, boxes, made, lists):
+    def kernel(lists, own, b0, b1, b2, b3, made, out):
+        out[...] = own[...] + ((b0[...] + b3[...]) + (b1[...] + b2[...]))
+
+        def add(j, carry):
+            fi = lanes(lists[2 * ROW + j])
+            out[:, fi] += made[j + 1, 0, 0:3, :]
+            si = lanes(lists[3 * ROW + j])
+            out[:, si] += made[j + 1, 1, 0:3, :]
+            return carry
+
+        lax.fori_loop(0, lists[6 * ROW + 1], add, 0)
+
+    vmem = pl.BlockSpec(memory_space=pltpu.VMEM)
+    return pl.pallas_call(
+        kernel,
+        out_shape=jax.ShapeDtypeStruct(own.shape, F32),
+        in_specs=[pl.BlockSpec(memory_space=pltpu.SMEM)] + [vmem] * 6,
+        out_specs=vmem,
+        compiler_params=pltpu.CompilerParams(vmem_limit_bytes=VMEM_LIMIT),
+    )(lists, own, *boxes, made)
 
 
 def body(positions, normals, areas, pair_first, pair_second, pair_count):
-    faces = areas.shape[0]
-    clusters = faces // C
-    me = lax.axis_index(("gx", "gy"))
-    geometry = jnp.concatenate([positions, normals, areas[None, :], jnp.zeros((1, faces), F32)], axis=0)
-    low, far, sib, high = gather(geometry, 7, 4)
-    first = pair_first - (me - REACH) * clusters
-    reach = pair_second // clusters - me
-    slot = REACH + jnp.where(jnp.abs(reach) == 1, reach * (1 - 2 * (me % 2)), reach)
-    second = slot * clusters + pair_second % clusters
-    outs = near_field(first, second, pair_count, [low, far, geometry, sib, high])
-    boxes = give_back(outs[0], outs[1], outs[3], outs[4])
-    return outs[2] + ((boxes[0] + boxes[3]) + (boxes[1] + boxes[2]))
+    geometry, lists = sort_out(positions, normals, areas, pair_first, pair_second, pair_count)
+    low, far, sib, high, early = gather(geometry, lists)
+    outs = near_field(lists, [low, far, geometry, sib, high], early, REACH)
+    *boxes, late = give_back(outs[0], outs[1], outs[3], outs[4], geometry, lists)
+    return finish(outs[2], boxes, late, lists)
 
 
 def solution(mesh):

time: 95.9 us -> 90.5 us (0.944)
  the two profiles are of different devices: /device:TPU:16 before, /device:TPU:8 now
where the time goes in v4:
time: 90.5 us; the launch traced here: 91 us
  Pallas kernels  90.3 us (100%)
    pallas_call x1, Pallas kernels, near_field(): pl.pallas_call(kernel, out_shape=[jax.ShapeDtypeStruct((3, faces), F32)]...  38.8 us
    pallas_call x1, Pallas kernels, gather(): pl.pallas_call(kernel, out_shape=[jax.ShapeDtypeStruct((clusters, 8, C),...  25.4 us
    pallas_call x1, Pallas kernels, give_back(): pl.pallas_call(kernel, out_shape=[jax.ShapeDtypeStruct((3, faces), F32)]...  18.5 us
    pallas_call x1, Pallas kernels, sort_out(): pl.pallas_call(kernel, out_shape=[jax.ShapeDtypeStruct((clusters, 8, C),...  5.12 us
    pallas_call x1, Pallas kernels, finish(): pl.pallas_call(kernel, out_shape=jax.ShapeDtypeStruct(own.shape, F32), in...  2.45 us

profile of v4, /device:TPU:8, one launch (start us, length us, event | category | flops | bytes accessed | tf_op | source)
XLA Modules:
  0.0 91.0 jit_solution(7285846120669576920)
XLA Ops:
  0.7 5.1 %shard_map.64 = (f32[64,8,256]{2,1,0:T(8,128)}, s32[896]{0:T(1024)}) custom-call(f32[3,16384]{1,0:T(4,128)} %pos.1, f32[3,16384]{1,0:T(4,128)} %nor.1, f32[1,16384]{1,0:T(1,128)} %bitcast.1, s32[128]{0:T(128)} %pf.1, s32[128]{0:T(128)} %ps.1, s32[1]{0:T(128)S(6)} %copy.7.count), custom_call_target="tpu_custom_call" | custom-call | tf_op jit(solution)/shard_map/pallas_call | solution.py:246
  5.8 25.4 %shard_map.65 = (f32[64,8,256]{2,1,0:T(8,128)}, f32[64,8,256]{2,1,0:T(8,128)}, f32[64,8,256]{2,1,0:T(8,128)}, f32[64,8,256]{2,1,0:T(8,128)}, f32[32,2,8,256]{3,2,1,0:T(8,128)}) custom-call(f32[64,8,256]{2,1,0:T(8,128)} %get-tuple-element.23.own.refs_2_, s32[896]{0:T(1024)} %get-tuple-element.22.lists), custom_call_target="tpu_custom_call" | custom-call | tf_op jit(solution)/shard_map/pallas_call | solution.py:327
  31.2 38.8 %shard_map.66 = (f32[3,16384]{1,0:T(4,128)}, f32[3,16384]{1,0:T(4,128)}, f32[3,16384]{1,0:T(4,128)}, f32[3,16384]{1,0:T(4,128)}, f32[3,16384]{1,0:T(4,128)}) custom-call(s32[896]{0:T(1024)} %get-tuple-element.22.lists, f32[32,2,8,256]{3,2,1,0:T(8,128)} %get-tuple-element.24.made, f32[64,8,256]{2,1,0:T(8,128)} %get-tuple-element.25.refs_0_, ...), custom_call_target="tpu_custom_call" | custom-call | tf_op jit(solution)/shard_map/pallas_call | solution.py:399
  70.0 18.5 %shard_map.67 = (f32[3,16384]{1,0:T(4,128)}, f32[3,16384]{1,0:T(4,128)}, f32[3,16384]{1,0:T(4,128)}, f32[3,16384]{1,0:T(4,128)}, f32[32,2,8,256]{3,2,1,0:T(8,128)}) custom-call(f32[3,16384]{1,0:T(4,128)} %get-tuple-element.30.low, f32[3,16384]{1,0:T(4,128)} %get-tuple-element.31.far, f32[3,16384]{1,0:T(4,128)} %get-tuple-element.32.sib, ...), custom_call_target="tpu_custom_call" | custom-call | tf_op jit(solution)/shard_map/pallas_call | solution.py:464
  88.5 2.4 %shard_map.68 = f32[3,16384]{1,0:T(4,128)} custom-call(s32[896]{0:T(1024)} %get-tuple-element.22.lists, f32[3,16384]{1,0:T(4,128)} %get-tuple-element.29.own, f32[3,16384]{1,0:T(4,128)} %get-tuple-element.34.b0, f32[3,16384]{1,0:T(4,128)} %get-tuple-element.35.b1, f32[3,16384]{1,0:T(4,128)} %get-tuple-element.36.b2, f32[3,16384]{1,0:T(4,128)} %get-tuple-element.37.b3, ...), custom_call_target="tpu_custom_call" | custom-call | tf_op jit(solution)/shard_map/pallas_call | solution.py:495
